TPU v7x, 256 devices: a whole 4x4x8 slice. The times are simulated.
256 devices in a mesh: users: 64 (over z, y, core), items: 4 (over x).
Axes of the slice: x: 4, y: 4, z: 8, core: 2. Of those that a mesh axis runs over, the one named last changes fastest.
Arguments:
- user_factor: bfloat16 [131072, 256], P('users'), may hold values from -2.390625 to 2.390625
- hot_factor: bfloat16 [512, 256], replicated, may hold values from -2.390625 to 2.390625
- cold_factor: bfloat16 [65536, 256], P(('users', 'items')), may hold values from -2.390625 to 2.390625
- hour_factor: bfloat16 [168, 256], replicated, may hold values from -2.390625 to 2.390625
- block_user: int32 [256, 512], P(('users', 'items')), may hold values from 0 to 2047
- block_slot: int32 [256, 512], P(('users', 'items')), may hold values from 0 to 159
- block_hour: int32 [256, 512], P(('users', 'items')), may hold values from 0 to 20
- block_count: int32 [256], P(('users', 'items')), may hold values from 128 to 512, as said below
- need_rows: int32 [256, 64, 2], P(('users', 'items')), may hold values from 0 to 15
- observed: bfloat16 [256, 512, 128], P(('users', 'items')), may hold values from 0 to 1, as said below
Outputs:
- user_grad: float32 [131072, 256], P(('users', 'items'))
- cold_grad: float32 [65536, 256], P(('users', 'items'))
- hot_grad: float32 [512, 256], P(('users', 'items'))
- hour_grad: float32 [168, 256], replicated
Inputs may be any that keep to these rules, and one draw needn't show every extreme that they name: `block_count`: some device has all 512 slots live. `observed`: every entry is 0 or 1.
All inputs are finite; a program needn't handle non-finite values.
Results may differ from a plain program's by a relative error of at most 0.0029.
Values may be sent and summed in bfloat16 or wider, within the bound.
A program may use at most 128 MiB of HBM per device.

v0:
```python
import jax
import jax.numpy as jnp
from jax import lax
from jax.sharding import PartitionSpec as P

IB = 16
HB = 8


def body(
    user_factor,
    hot_factor,
    cold_factor,
    hour_factor,
    block_user,
    block_slot,
    block_hour,
    block_count,
    need_rows,
    observed,
):
    rank_size = user_factor.shape[1]
    hour_count = hour_factor.shape[0]
    hour_blocks = hour_count // HB
    hot_rows = hot_factor.shape[0]
    shard_len = cold_factor.shape[0]
    peer_count = lax.axis_size("users")
    requests = need_rows[0]
    offsets = jnp.arange(IB, dtype=jnp.int32)
    gathered = lax.all_gather(cold_factor, "users", axis=0, tiled=True)
    wanted_rows = (
        jnp.arange(peer_count, dtype=jnp.int32)[:, None, None] * shard_len
        + requests[:, :, None] * IB
        + offsets
    ).reshape(-1)
    fetched = gathered[wanted_rows]
    item_table = jnp.concatenate([hot_factor, fetched], axis=0)
    hour_table = hour_factor.reshape(hour_blocks, HB * rank_size)
    block_total = block_user.shape[1]
    group_len = min(block_total, 512)
    groups = block_total // group_len
    live_count = block_count[0]
    data = (
        block_user[0].reshape(groups, group_len),
        block_slot[0].reshape(groups, group_len),
        block_hour[0].reshape(groups, group_len),
        jnp.arange(block_total, dtype=jnp.int32).reshape(groups, group_len),
        observed[0].reshape(groups, group_len, IB, HB),
    )
    block_ids = jnp.arange(hour_blocks, dtype=jnp.int32)

    def one_group(carry, group_data):
        grad_user, grad_item, grad_hour = carry
        users_idx, slots_idx, hours_idx, position, obs = group_data
        user_rows = user_factor[users_idx]
        item_idx = slots_idx[:, None] * IB + offsets
        item_rows = item_table[item_idx]
        hour_onehot = (hours_idx[:, None] == block_ids).astype(jnp.bfloat16)
        hour_rows = jnp.dot(hour_onehot, hour_table, preferred_element_type=jnp.float32)
        hour_rows = hour_rows.astype(jnp.bfloat16).reshape(group_len, HB, rank_size)
        user_item = (
            user_rows.astype(jnp.float32)[:, None, :] * item_rows.astype(jnp.float32)
        ).astype(jnp.bfloat16)
        model = jnp.einsum("gar,gbr->gab", user_item, hour_rows, preferred_element_type=jnp.float32)
        live_mask = position < live_count
        residual = jnp.where(
            live_mask[:, None, None], jax.nn.sigmoid(model) - obs.astype(jnp.float32), 0.0
        )
        residual = residual.astype(jnp.bfloat16)
        weighted = jnp.einsum(
            "gab,gbr->gar", residual, hour_rows, preferred_element_type=jnp.float32
        )
        item_terms = weighted * user_rows.astype(jnp.float32)[:, None, :]
        user_terms = jnp.sum(weighted * item_rows.astype(jnp.float32), axis=1)
        hour_terms = jnp.einsum(
            "gab,gar->gbr", residual, user_item, preferred_element_type=jnp.float32
        )
        grad_user = grad_user.at[users_idx].add(user_terms)
        grad_item = grad_item.at[item_idx.reshape(-1)].add(item_terms.reshape(-1, rank_size))
        grad_hour = grad_hour.at[hours_idx].add(hour_terms.reshape(group_len, HB * rank_size))
        return ((grad_user, grad_item, grad_hour), None)

    start = (
        jnp.zeros((user_factor.shape[0], rank_size), jnp.float32),
        jnp.zeros((item_table.shape[0], rank_size), jnp.float32),
        jnp.zeros((hour_blocks, HB * rank_size), jnp.float32),
    )
    (grad_user, grad_item, grad_hour), _ = lax.scan(one_group, start, data)
    cold_part = grad_item[hot_rows:]
    dense_terms = (
        jnp.zeros((peer_count * shard_len, rank_size), jnp.float32).at[wanted_rows].add(cold_part)
    )
    cold_grad = lax.psum_scatter(dense_terms, "users", scatter_dimension=0, tiled=True)
    hot_grad = lax.psum_scatter(
        grad_item[:hot_rows], ("users", "items"), scatter_dimension=0, tiled=True
    )
    user_grad = lax.psum_scatter(grad_user, "items", scatter_dimension=0, tiled=True)
    hour_grad = lax.psum(grad_hour, ("users", "items")).reshape(hour_count, rank_size)
    return (user_grad, cold_grad, hot_grad, hour_grad)


def solution(mesh):
    in_specs = (
        P("users", None),
        P(),
        P(("users", "items"), None),
        P(),
        P(("users", "items"), None),
        P(("users", "items"), None),
        P(("users", "items"), None),
        P(("users", "items")),
        P(("users", "items"), None, None),
        P(("users", "items"), None, None),
    )
    out_specs = (
        P(("users", "items"), None),
        P(("users", "items"), None),
        P(("users", "items"), None),
        P(),
    )
    return jax.shard_map(body, mesh=mesh, in_specs=in_specs, out_specs=out_specs, check_vma=False)
```

profile of v0, /device:TPU:6, one launch (start us, length us, event | category | flops | bytes accessed | tf_op | source)
XLA Modules:
  0.0 702.9 jit_solution(4450357891006991247)
XLA Ops:
  7.2 0.0 copy-start
  7.2 0.0 copy-start.6
  7.2 0.0 all-gather.2.cloned.1.call-start
  7.2 0.7 all-gather.2.cloned.1.call-update
  7.9 0.0 all-reduce.4.cloned.1.call-start
  8.6 0.7 bitcast_add_fusion
  9.3 0.1 copy.18
  9.4 0.1 iota_add_fusion.1
  9.5 0.1 add.165
  9.7 1.0 reshape.237
  10.7 1.0 copy.19
  11.7 0.7 compare_select_fusion.4
  12.4 2.0 gather_fusion
  14.3 0.0 copy-start.5
  14.4 0.1 iota_add_fusion
  14.6 0.1 add.175
  14.7 0.1 compare_select_fusion
  14.8 0.1 reshape.261
  15.0 2.0 copy.20
  17.0 0.8 convolution_convert_fusion
  17.8 2.1 copy.21
  19.9 0.0 copy-start.4
  19.9 76.8 %all-gather.2.cloned.1.call-done = bf16[16384,256]{1,0:T(8,128)(2,1)} async-done(((bf16[256,256]{1,0:T(8,128)(2,1)}), bf16[16384,256]{1,0:T(8,128)(2,1)}) %all-gather.2.cloned.1.call-update) | async-done | bytes 8388624 | tf_op jit(solution)/shard_map/all_gather | solution.py:30
  96.7 11.1 %gather_fusion.1 = bf16[2048,256]{1,0:T(8,128)(2,1)S(1)} fusion(bf16[16384,256]{1,0:T(8,128)(2,1)} %all-gather.2.cloned.1.call-done, s32[2048]{0:T(1024)S(1)} %broadcast_clamp_fusion.1), kind=kCustom, calls=%fused_computation.1 | custom fusion | bytes 2105344 | tf_op jit(solution)/shard_map/gather | solution.py:36
  107.8 0.1 pad_maximum_fusion
  107.9 32.9 %gather_fusion.2 = bf16[8192,256]{1,0:T(8,128)(2,1)} fusion(bf16[2560,256]{1,0:T(8,128)(2,1)S(1)} %pad_maximum_fusion, s32[8192]{0:T(1024)S(1)} %broadcast_clamp_fusion), kind=kCustom, calls=%fused_computation.2 | custom fusion | bytes 8421376 | tf_op jit(solution)/shard_map/while/body/eval_jaxpr/gather | solution.py:57
  140.8 5.0 select_convert_fusion
  145.9 1.0 fusion.4
  146.8 0.6 copy-done.3
  147.5 5.1 broadcast_multiply_fusion
  152.6 3.9 copy.22
  156.5 8.7 %scatter_custom_fusion.3 = f32[21,2048]{1,0:T(8,128)S(1)} fusion(s32[512]{0:T(512)S(1)} %bitcast.48, f32[512,2048]{1,0:T(8,128)} %bitcast.39, f32[]{:T(128)} %constant.13.clone.1), kind=kCustom, calls=%fused_computation.30 | custom fusion | flops 1048576 | bytes 172544 | tf_op jit(solution)/shard_map/while/body/eval_jaxpr/scatter-add | solution.py:80
  165.2 0.7 reshape.241
  165.9 46.2 %scatter_custom_fusion.1 = f32[2560,256]{1,0:T(8,128)} fusion(s32[8192]{0:T(1024)S(1)} %bitcast.40, f32[8192,256]{1,0:T(8,128)} %bitcast.35, f32[]{:T(128)} %constant.13.clone.1), kind=kCustom, calls=%fused_computation.20 | custom fusion | flops 2097152 | bytes 2621952 | tf_op jit(solution)/shard_map/while/body/eval_jaxpr/scatter-add | solution.py:79
  212.1 1.9 slice.15
  214.0 0.0 all-reduce.4.cloned.1.call-update
  214.0 0.0 reduce-scatter.3.cloned.1.call-start
  214.1 4.9 scatter_custom_fusion
  219.0 0.0 reduce-scatter.3.cloned.1.call-update
  219.0 0.0 reduce-scatter.5.cloned.1.call-start
  219.1 18.9 %scatter_custom_fusion.2 = f32[16384,256]{1,0:T(8,128)} fusion(s32[2048]{0:T(1024)S(1)} %bitcast.42, f32[]{:T(128)} %constant.13.clone.1, f32[2560,256]{1,0:T(8,128)} %scatter_custom_fusion.1), kind=kCustom, calls=%fused_computation.11 | custom fusion | flops 524288 | bytes 18874880 | tf_op jit(solution)/shard_map/scatter-add | solution.py:91
  237.9 0.0 reduce-scatter.5.cloned.1.call-update
  238.0 0.0 copy-start.1
  238.0 229.4 %all-reduce.4.cloned.1.call-done = (f32[512,256]{1,0:T(8,128)}, f32[168,256]{1,0:T(8,128)}) async-done(((f32[512,256]{1,0:T(8,128)}, f32[168,256]{1,0:T(8,128)}), (f32[512,256]{1,0:T(8,128)}, f32[168,256]{1,0:T(8,128)})) %all-reduce.4.cloned.1.call-update) | async-done | bytes 696336
  467.4 1.3 constant_dynamic-slice_fusion
  468.6 29.8 %reduce-scatter.3.cloned.1.call-done = f32[512,256]{1,0:T(8,128)} async-done(((f32[2048,256]{1,0:T(8,128)}), f32[512,256]{1,0:T(8,128)}) %reduce-scatter.3.cloned.1.call-update) | async-done | bytes 524304 | tf_op jit(solution)/shard_map/reduce_scatter | solution.py:97
  498.4 196.4 %reduce-scatter.5.cloned.1.call-done = f32[256,256]{1,0:T(8,128)} async-done(((f32[16384,256]{1,0:T(8,128)}), f32[256,256]{1,0:T(8,128)}) %reduce-scatter.5.cloned.1.call-update) | async-done | bytes 262160 | tf_op jit(solution)/shard_map/reduce_scatter | solution.py:93
  694.8 1.6 copy.26
  (19 shorter events, 0.2 us)
Async XLA Ops:
  7.2 5.2 copy-start
  7.2 7.2 %copy-start.6 = (s32[1,512]{1,0:T(1,128)S(1)}, s32[1,512]{1,0:T(1,128)}, u32[]{:S(2)}) copy-start(s32[1,512]{1,0:T(1,128)} %param.15) | copy-start | bytes 6148
  7.2 89.5 %all-gather.2.cloned.1.call-start = ((), (), s32[]{:S(2)}) async-start(), calls=%async_computation.2 | async-start | bytes 8519680 | tf_op jit(solution)/shard_map/all_gather | solution.py:30
  7.9 459.4 %all-reduce.4.cloned.1.call-start = ((), (), s32[]{:S(2)}) async-start(), calls=%async_computation.5 | async-start | bytes 1392640
  14.3 2.7 copy-start.5
  19.9 87.9 %copy-start.4 = (bf16[512,256]{1,0:T(8,128)(2,1)S(1)}, bf16[512,256]{1,0:T(8,128)(2,1)}, u32[]{:S(2)}) copy-start(bf16[512,256]{1,0:T(8,128)(2,1)} %param.11) | copy-start | bytes 786436
  140.8 5.0 copy-start.2
  145.9 1.6 copy-start.3
  214.0 284.4 %reduce-scatter.3.cloned.1.call-start = ((), (), s32[]{:S(2)}) async-start(), calls=%async_computation.3 | async-start | bytes 2621440 | tf_op jit(solution)/shard_map/reduce_scatter | solution.py:97
  219.0 475.8 %reduce-scatter.5.cloned.1.call-start = ((), (), s32[]{:S(2)}) async-start(), calls=%async_computation.4 | async-start | bytes 17039360 | tf_op jit(solution)/shard_map/reduce_scatter | solution.py:93
  238.0 458.4 %copy-start.1 = (bf16[2048,256]{1,0:T(8,128)(2,1)S(1)}, bf16[2048,256]{1,0:T(8,128)(2,1)}, u32[]{:S(2)}) copy-start(bf16[2048,256]{1,0:T(8,128)(2,1)} %param.10) | copy-start | bytes 3145732
Sparse Core Ops, SparseCore 0:
  10.8 85.8 all-gather.1
  214.2 253.1 all-reduce.3
  470.5 27.8 reduce-scatter.2
  503.3 191.4 reduce-scatter.4
where the time goes:
time: 703 us
  waiting for transfers between devices  533 us (76%)
  other arithmetic  80.7 us (11%)
  local copies, waits for them, and re-layouts  62.5 us (9%)
  between operations  14.7 us (2%)
  matrix products  11.9 us (2%)
    unnamed x5, waiting for transfers between devices  230 us
    reduce_scatter x1, waiting for transfers between devices, body(): lax.psum_scatter(dense_terms, 'users', scatter_dimension=0, tiled=True)  196 us
    all_gather x1, waiting for transfers between devices, body(): gathered = lax.all_gather(cold_factor, 'users', axis=0, tiled=True)  76.8 us
    scatter-add x1, other arithmetic, one_group(): grad_item.at[item_idx.reshape(-1)].add(item_terms.reshape(-1, rank_size))  46.2 us
    gather x1, local copies, waits for them, and re-layouts, one_group(): item_rows = item_table[item_idx]  32.9 us
    reduce_scatter x1, waiting for transfers between devices, body(): lax.psum_scatter(grad_user, 'items', scatter_dimension=0, tiled=True)  29.8 us
    scatter-add x1, other arithmetic, body(): jnp.zeros((peer_count * shard_len, rank_size), jnp.float32).at[wanted_rows]  18.9 us
  transfers between devices with their start and end apart: 4, of which 4 were waited for; matrix products, arithmetic and copies ran while one was open for 5% of the time, Pallas kernels for 0%

commit v1 on v0

--- a/solution.py
+++ b/solution.py
@@ -27,7 +27,9 @@
     peer_count = lax.axis_size("users")
     requests = need_rows[0]
     offsets = jnp.arange(IB, dtype=jnp.int32)
-    gathered = lax.all_gather(cold_factor, "users", axis=0, tiled=True)
+    gathered = jnp.concatenate(
+        lax.all_to_all(jnp.stack([cold_factor] * lax.axis_size("users")), "users", 0, 0), axis=0
+    )
     wanted_rows = (
         jnp.arange(peer_count, dtype=jnp.int32)[:, None, None] * shard_len
         + requests[:, :, None] * IB

time: 703 us -> 610 us (0.87)
  waiting for transfers between devices: 533 us -> 420 us
  starting transfers between devices: 0.16 us -> 12.9 us
    reduce_scatter x1, waiting for transfers between devices: 196 us -> 0.01 us  [body(): lax.psum_scatter(dense_terms, 'users', scatter_dimension=0, tiled=True)]
    all_to_all x0 -> x1, waiting for transfers between devices: none -> 177 us  [body(): lax.all_to_all(jnp.stack([cold_factor] * lax.axis_size('users')), 'users'...]
    all_gather x1 -> x0, waiting for transfers between devices: 76.8 us -> none  [body(): gathered = lax.all_gather(cold_factor, 'users', axis=0, tiled=True)]
    reduce_scatter x1, waiting for transfers between devices: 29.8 us -> 0.01 us  [body(): lax.psum_scatter(grad_user, 'items', scatter_dimension=0, tiled=True)]
    all_to_all x0 -> x1, starting transfers between devices: none -> 12.5 us  [body(): lax.all_to_all(jnp.stack([cold_factor] * lax.axis_size('users')), 'users'...]
    unnamed x5 -> x4, waiting for transfers between devices: 230 us -> 242 us
  transfers between devices with their start and end apart: 4 -> 4, of which waited for: 4 -> 2; matrix products, arithmetic and copies ran while one was open for 5% -> 5% of each run, Pallas kernels for 0% -> 0%
where the time goes in v1:
time: 610 us
  waiting for transfers between devices  420 us (69%)
  other arithmetic  79 us (13%)
  local copies, waits for them, and re-layouts  67.8 us (11%)
  between operations  16.5 us (3%)
  matrix products  13.8 us (2%)
  starting transfers between devices  12.9 us (2%)
    unnamed x4, waiting for transfers between devices  242 us
    all_to_all x1, waiting for transfers between devices, body(): lax.all_to_all(jnp.stack([cold_factor] * lax.axis_size('users')), 'users'...  177 us
    scatter-add x1, other arithmetic, one_group(): grad_item.at[item_idx.reshape(-1)].add(item_terms.reshape(-1, rank_size))  46.2 us
    gather x1, local copies, waits for them, and re-layouts, one_group(): item_rows = item_table[item_idx]  32.9 us
    scatter-add x1, other arithmetic, body(): jnp.zeros((peer_count * shard_len, rank_size), jnp.float32).at[wanted_rows]  18.9 us
    all_to_all x1, starting transfers between devices, body(): lax.all_to_all(jnp.stack([cold_factor] * lax.axis_size('users')), 'users'...  12.5 us
  transfers between devices with their start and end apart: 4, of which 2 were waited for; matrix products, arithmetic and copies ran while one was open for 5% of the time, Pallas kernels for 0%

profile of v1, /device:TPU:6, one launch (start us, length us, event | category | flops | bytes accessed | tf_op | source)
XLA Modules:
  0.0 609.6 jit_solution(15623193032223122686)
XLA Ops:
  8.0 0.0 copy-start
  8.0 5.2 stack.2
  13.2 12.5 %all-to-all-start = ((bf16[64,256,256]{2,1,0:T(8,128)(2,1)}), bf16[64,256,256]{2,1,0:T(8,128)(2,1)}, u32[]{:S(2)}, u32[]{:S(2)}) async-start(bf16[64,256,256]{2,1,0:T(8,128)(2,1)} %stack.2), calls=%async_computation | async-start | bytes 16777216 | tf_op jit(solution)/shard_map/all_to_all | solution.py:31
  25.7 0.0 copy-start.6
  25.8 0.0 copy-start.7
  25.8 0.0 all-reduce.4.cloned.1.call-start
  25.8 0.0 copy-done.10
  25.9 0.1 copy.18
  26.0 0.1 iota_add_fusion.1
  26.1 0.1 add.165
  26.2 0.0 copy-done.8
  26.2 0.1 compare_select_fusion
  26.4 0.1 reshape.267
  26.6 2.0 gather_fusion
  28.6 0.0 copy-done.6
  28.6 0.1 reshape.243
  28.7 0.0 copy-done.7
  28.7 0.8 convolution_convert_fusion
  29.4 0.0 copy-start.5
  29.4 2.0 copy.21
  31.5 0.1 copy.19
  31.6 2.0 copy.20
  34.3 0.1 iota_add_fusion
  34.4 0.1 add.175
  34.7 177.3 %all-to-all-done = bf16[64,256,256]{2,1,0:T(8,128)(2,1)} async-done(((bf16[64,256,256]{2,1,0:T(8,128)(2,1)}), bf16[64,256,256]{2,1,0:T(8,128)(2,1)}, u32[]{:S(2)}, u32[]{:S(2)}) %all-to-all-start) | async-done | bytes 8388640 | tf_op jit(solution)/shard_map/all_to_all | solution.py:31
  211.9 11.1 %gather_fusion.1 = bf16[2048,256]{1,0:T(8,128)(2,1)S(1)} fusion(bf16[16384,256]{1,0:T(8,128)(2,1)} %bitcast.3, s32[2048]{0:T(1024)S(1)} %broadcast_clamp_fusion.1), kind=kCustom, calls=%fused_computation.1 | custom fusion | bytes 2105344 | tf_op jit(solution)/shard_map/gather | solution.py:38
  223.1 0.1 pad_maximum_fusion
  223.2 32.9 %gather_fusion.2 = bf16[8192,256]{1,0:T(8,128)(2,1)} fusion(bf16[2560,256]{1,0:T(8,128)(2,1)S(1)} %pad_maximum_fusion, s32[8192]{0:T(1024)S(1)} %broadcast_clamp_fusion), kind=kCustom, calls=%fused_computation.2 | custom fusion | bytes 8421376 | tf_op jit(solution)/shard_map/while/body/eval_jaxpr/gather | solution.py:59
  256.1 5.0 select_convert_fusion
  261.2 0.2 copy-done.3
  261.4 5.1 broadcast_multiply_fusion
  266.5 2.9 fusion.4
  269.4 46.2 %scatter_custom_fusion.1 = f32[2560,256]{1,0:T(8,128)} fusion(s32[8192]{0:T(1024)S(1)} %bitcast.41, f32[8192,256]{1,0:T(8,128)} %bitcast.36, f32[]{:T(128)} %constant.13.clone.1), kind=kCustom, calls=%fused_computation.20 | custom fusion | flops 2097152 | bytes 2621952 | tf_op jit(solution)/shard_map/while/body/eval_jaxpr/scatter-add | solution.py:81
  315.7 1.9 slice.15
  317.6 6.1 copy.22
  323.6 8.5 %scatter_custom_fusion.3 = f32[21,2048]{1,0:T(8,128)S(1)} fusion(s32[512]{0:T(512)S(1)} %bitcast.49, f32[512,2048]{1,0:T(8,128)} %bitcast.40, f32[]{:T(128)} %constant.13.clone.1), kind=kCustom, calls=%fused_computation.30 | custom fusion | flops 1048576 | bytes 172544 | tf_op jit(solution)/shard_map/while/body/eval_jaxpr/scatter-add | solution.py:82
  332.1 0.7 reshape.247
  332.8 0.0 all-reduce.4.cloned.1.call-update
  332.9 0.0 reduce-scatter.3.cloned.1.call-start
  332.9 4.7 scatter_custom_fusion
  337.6 0.0 reduce-scatter.3.cloned.1.call-update
  337.6 0.3 reduce-scatter.5.cloned.1.call-start
  337.9 18.9 %scatter_custom_fusion.2 = f32[16384,256]{1,0:T(8,128)} fusion(s32[2048]{0:T(1024)S(1)} %bitcast.43, f32[]{:T(128)} %constant.13.clone.1, f32[2560,256]{1,0:T(8,128)} %scatter_custom_fusion.1), kind=kCustom, calls=%fused_computation.11 | custom fusion | flops 524288 | bytes 18874880 | tf_op jit(solution)/shard_map/scatter-add | solution.py:93
  356.8 0.0 reduce-scatter.5.cloned.1.call-update
  356.9 0.0 copy-start.1
  356.9 242.4 %all-reduce.4.cloned.1.call-done = (f32[512,256]{1,0:T(8,128)}, f32[168,256]{1,0:T(8,128)}) async-done(((f32[512,256]{1,0:T(8,128)}, f32[168,256]{1,0:T(8,128)}), (f32[512,256]{1,0:T(8,128)}, f32[168,256]{1,0:T(8,128)})) %all-reduce.4.cloned.1.call-update) | async-done | bytes 696336
  599.3 1.3 constant_dynamic-slice_fusion
  600.6 1.6 copy.26
  (27 shorter events, 0.2 us)
Async XLA Ops:
  8.0 18.6 %copy-start = (bf16[2048,256]{1,0:T(8,128)(2,1)S(1)}, bf16[2048,256]{1,0:T(8,128)(2,1)}, u32[]{:S(2)}) copy-start(bf16[2048,256]{1,0:T(8,128)(2,1)} %param.10) | copy-start | bytes 3145732
  13.2 12.6 %copy-start.10 = (s32[1,64,2]{1,2,0:T(2,128)S(1)}, s32[1,64,2]{1,2,0:T(2,128)}, u32[]{:S(2)}) copy-start(s32[1,64,2]{1,2,0:T(2,128)} %param.18) | copy-start | bytes 1540
  13.2 13.0 %copy-start.8 = (s32[1,512]{1,0:T(1,128)S(1)}, s32[1,512]{1,0:T(1,128)}, u32[]{:S(2)}) copy-start(s32[1,512]{1,0:T(1,128)} %param.15) | copy-start | bytes 6148
  13.2 13.3 %copy-start.9 = (s32[1,512]{1,0:T(1,128)S(1)}, s32[1,512]{1,0:T(1,128)}, u32[]{:S(2)}) copy-start(s32[1,512]{1,0:T(1,128)} %param.14) | copy-start | bytes 6148
  13.2 198.7 %all-to-all-start = ((bf16[64,256,256]{2,1,0:T(8,128)(2,1)}), bf16[64,256,256]{2,1,0:T(8,128)(2,1)}, u32[]{:S(2)}, u32[]{:S(2)}) async-start(bf16[64,256,256]{2,1,0:T(8,128)(2,1)} %stack.2), calls=%async_computation | async-start | bytes 16777216 | tf_op jit(solution)/shard_map/all_to_all | solution.py:31
  25.7 2.8 copy-start.6
  25.8 2.9 copy-start.7
  25.8 573.6 %all-reduce.4.cloned.1.call-start = ((), (), s32[]{:S(2)}) async-start(), calls=%async_computation.5 | async-start | bytes 1392640
  29.4 2.0 copy-start.5
  211.9 11.2 %copy-start.4 = (bf16[512,256]{1,0:T(8,128)(2,1)S(1)}, bf16[512,256]{1,0:T(8,128)(2,1)}, u32[]{:S(2)}) copy-start(bf16[512,256]{1,0:T(8,128)(2,1)} %param.11) | copy-start | bytes 786436
  256.1 5.0 copy-start.2
  256.1 5.3 copy-start.3
  332.9 267.8 %reduce-scatter.3.cloned.1.call-start = ((), (), s32[]{:S(2)}) async-start(), calls=%async_computation.3 | async-start | bytes 2621440 | tf_op jit(solution)/shard_map/reduce_scatter | solution.py:99
  337.6 263.0 %reduce-scatter.5.cloned.1.call-start = ((), (), s32[]{:S(2)}) async-start(), calls=%async_computation.4 | async-start | bytes 17039360 | tf_op jit(solution)/shard_map/reduce_scatter | solution.py:95
  356.9 245.3 %copy-start.1 = (bf16[2048,256]{1,0:T(8,128)(2,1)S(1)}, bf16[2048,256]{1,0:T(8,128)(2,1)}, u32[]{:S(2)}) copy-start(bf16[2048,256]{1,0:T(8,128)(2,1)} %param.10) | copy-start | bytes 3145732
Sparse Core Ops, SparseCore 0:
  333.0 266.3 all-reduce.3
Sparse Core Ops, SparseCore 1:
  337.7 27.5 reduce-scatter.2
  370.2 191.6 reduce-scatter.4
